TPU v7x, 128 devices: a whole 4x4x4 slice. The times are simulated.
128 devices in a mesh: cls: 4 (over y_lo, core), grp: 32 (over x, y_hi, z).
Axes of the slice: x: 4, y: 4 (y_hi: 2, y_lo: 2; y = y_hi * 2 + y_lo), z: 4, core: 2. Of those that a mesh axis runs over, the one named last changes fastest.
Arguments:
- images: bfloat16 [1024, 9216], P(('cls', 'grp')), may hold values from -40 to 40
- ctf: bfloat16 [1024, 64], P(('cls', 'grp')), may hold values from -1 to 1
- refs: bfloat16 [512, 9216], P('cls'), may hold values from -12 to 12
- noise_inv: float32 [64], replicated, may hold values from 0.006 to 0.024
- reg: float32 [64], replicated, may hold values from 0.01 to 0.1
Outputs:
- new_refs: float32 [512, 9216], P('cls')
All inputs are finite; a program needn't handle non-finite values.
Results may differ from a plain program's by a relative error of at most 0.004.
Values may be sent and summed in bfloat16 or wider, within the bound.
A program may use at most 192 MiB of HBM per device.

v0:
```python
import jax
import jax.numpy as jnp
from jax import lax
from jax.experimental import pallas as pl
from jax.experimental.pallas import tpu as pltpu
from jax.sharding import PartitionSpec as P

MESH = pl.DeviceIdType.MESH
BF16 = jnp.bfloat16
F32 = jnp.float32
HIGHEST = lax.Precision.HIGHEST

CYCLES = 64
PIX = 9216
ROWS = 8
SLOTS = 8
PART = 64
HALF = 64
BLOCKS = 36
WIDE = 256
TURN = 4
SHIFT = 9
PIECE = 16
QUARTER = PIX // 4
FULL = QUARTER + 256
CUT = FULL // 2
CHUNKS = 3
CHUNK = PIX // CHUNKS
PER = BLOCKS // CHUNKS
STEP = 3


def ring(v, step):
    return lax.rem(v + step, 4)


def device(x, y, z, core):
    return (lax.rem(y, 2) * 2 + core, x * 8 + lax.div(y, 2) * 4 + z)


def dot_nt(a, b, precision=None):
    return lax.dot_general(a, b, (((1,), (1,)), ((), ())), precision=precision, preferred_element_type=F32)


def dot_nn(a, b, precision=None):
    return lax.dot_general(a, b, (((1,), (0,)), ((), ())), precision=precision, preferred_element_type=F32)


def twice(v):
    return jnp.concatenate([v, v], axis=1)


def split(v):
    high = v.astype(BF16)
    return high, (v - high.astype(F32)).astype(BF16)


def remote(src, dst, send, recv, target):
    return pltpu.make_async_remote_copy(
        src_ref=src, dst_ref=dst, send_sem=send, recv_sem=recv, device_id=target, device_id_type=MESH
    )


def kernel(images, ctf, refs, noise_hbm, reg_hbm, out, gathered, ctfs, blocks, classes, noise, reg, factors, curves,
           squares, powers, cross, weights, stats, own_stats, numer, bottoms, parts, far_low, far_high, plain, summed,
           fwd, total, total_bottom, ready, two_a, two_b, two_c, two_d, two_e, two_f, two_fa, two_fb, pieces,
           img_send, img_recv, ctf_send, ctf_recv, st_send, st_recv, loc_sem, ref_sem, rs_send, rs_recv, ag_send, ag_recv):
    cls = lax.axis_index("cls")
    grp = lax.axis_index("grp")
    core = lax.rem(cls, 2)
    x = lax.div(grp, 8)
    z = lax.rem(grp, 4)
    y_hi = lax.rem(lax.div(grp, 4), 2)
    y = y_hi * 2 + lax.div(cls, 2)
    me = y * 2 + core
    up, down, far = ring(y, 1), ring(y, 3), ring(y, 2)
    q1 = x + core * (z - x)
    q2 = z + core * (x - z)

    def at(v1, v2):
        return device(v1 + core * (v2 - v1), y, v2 + core * (v1 - v2), core)

    right1, left1, opp1 = ring(q1, 1), ring(q1, 3), ring(q1, 2)
    right2, left2, opp2 = ring(q2, 1), ring(q2, 3), ring(q2, 2)
    to_r1, to_l1 = at(right1, q2), at(left1, q2)
    to_r2, to_l2 = at(q1, right2), at(q1, left2)
    to_y = device(x, far, z, core)

    def peer(o):
        slot = lax.rem(me + o, SLOTS)
        return device(x, lax.div(slot, 2), z, lax.rem(slot, 2))

    barrier = pltpu.get_barrier_semaphore()
    for o in range(1, SLOTS):
        pl.semaphore_signal(barrier, inc=1, device_id=peer(o), device_id_type=MESH)
    for target in (to_r1, to_l1, to_r2, to_l2):
        pl.semaphore_signal(barrier, inc=1, device_id=target, device_id_type=MESH)

    local = [
        pltpu.make_async_copy(images, gathered.at[me], loc_sem.at[0]),
        pltpu.make_async_copy(ctf, ctfs.at[me], loc_sem.at[1]),
        pltpu.make_async_copy(noise_hbm, noise, loc_sem.at[2]),
        pltpu.make_async_copy(reg_hbm, reg, loc_sem.at[3]),
    ]
    for copy in local:
        copy.start()
    first = pl.multiple_of(y_hi * HALF, HALF)
    ref_copies = []
    for j in range(4):
        for m in range(2 * SHIFT - 1):
            b = (4 * m + j) % BLOCKS
            ref_copies.append(pltpu.make_async_copy(
                refs.at[pl.ds(first, HALF), pl.ds(b * WIDE, WIDE)], classes.at[j, m], ref_sem.at[len(ref_copies)]))
            ref_copies[-1].start()

    pl.semaphore_wait(barrier, SLOTS + 3)

    sibling = device(x, y, z, 1 - core)
    above = device(x, up, z, core)
    below = device(x, down, z, core)
    slot_down, slot_up, slot_far = down * 2 + core, up * 2 + core, far * 2 + core
    moves = {}

    def move(c, i):
        if i < 3:
            slot, lo, size, target = me, 0, CHUNK, (above, below, sibling)[i]
        elif i == 3:
            slot, lo, size, target = slot_down, 0, CHUNK // 2, above
        elif i == 4:
            slot, lo, size, target = slot_down, 0, CHUNK, sibling
        elif i == 5:
            slot, lo, size, target = slot_up, CHUNK // 2, CHUNK // 2, below
        elif i == 6:
            slot, lo, size, target = slot_up, 0, CHUNK, sibling
        else:
            slot, lo, size, target = slot_far, (i - 7) * (CHUNK // 2), CHUNK // 2, sibling
        lanes = pl.ds(c * CHUNK + lo, size)
        src = images.at[:, lanes] if i < 3 else gathered.at[slot, :, lanes]
        moves[c, i] = remote(src, gathered.at[slot, :, lanes], img_send.at[9 * c + i], img_recv.at[9 * c + i], target)
        moves[c, i].start()

    def neighbours(c):
        moves[c, 0].wait_recv()
        move(c, 3)
        move(c, 4)
        moves[c, 1].wait_recv()
        move(c, 5)
        move(c, 6)

    def distant(c):
        moves[c, 3].wait_recv()
        move(c, 7)
        moves[c, 5].wait_recv()
        move(c, 8)

    def complete(c):
        for i in (2, 4, 6, 7, 8):
            moves[c, i].wait_recv()

    move(0, 0)
    move(0, 1)
    move(1, 0)
    move(1, 1)
    ctf_copies = [remote(ctf, ctfs.at[me], ctf_send.at[o - 1], ctf_recv.at[o - 1], peer(o)) for o in range(1, SLOTS)]
    for copy in ctf_copies:
        copy.start()
    move(0, 2)
    cross[...] = jnp.zeros_like(cross)
    squares[...] = jnp.zeros_like(squares)
    for copy in local:
        copy.wait()
    neighbours(0)
    move(2, 0)
    move(2, 1)
    move(1, 2)
    move(2, 2)
    for copy in ref_copies:
        copy.wait()
    powers[...] = jnp.zeros_like(powers)

    @pl.loop(0, SHIFT)
    def _(m):
        value = powers[...]
        for j in range(4):
            v = classes[j, m].astype(F32)
            v = v * v
            value = value + (v[:, :128] + v[:, 128:])
        powers[...] = value

    for copy in ctf_copies:
        copy.wait_recv()
    noise_row = noise[...]
    for slot in range(SLOTS):
        value = ctfs[slot].astype(F32)
        factor = value * noise_row
        factors[pl.ds(slot * ROWS, ROWS), :] = twice(factor)
        curves[pl.ds(slot * ROWS, ROWS), :] = twice(factor * value)

    def prepare(c):
        @pl.loop(c * PER, (c + 1) * PER)
        def _(b):
            lanes = pl.ds(pl.multiple_of(b * WIDE, WIDE), WIDE)
            for level in range(4):
                weighted = []
                for core_slot in range(2):
                    slot = level * 2 + core_slot
                    rows = pl.ds(slot * ROWS, ROWS)
                    value = gathered[slot, :, lanes].astype(F32)
                    square = value * value
                    squares[rows, :] += square[:, :128] + square[:, 128:]
                    weighted.append(value * twice(factors[rows, :]))
                blocks[b, pl.ds(level * 2 * ROWS, 2 * ROWS), :] = jnp.concatenate(weighted, axis=0).astype(BF16)

    def score(start, stop):
        @pl.loop(start // STEP, stop // STEP)
        def _(u):
            left, right = [], []
            for v in range(STEP):
                b = u * STEP + v
                left.append(classes[lax.rem(b, 4), pl.ds(lax.div(b, 4), SHIFT)].reshape(SHIFT * HALF, WIDE))
                right.append(blocks[pl.ds(b, TURN)].reshape(TURN * PART, WIDE))
            cross[...] += dot_nt(jnp.concatenate(left, axis=1), jnp.concatenate(right, axis=1))

    neighbours(1)
    distant(0)
    complete(0)
    neighbours(2)
    distant(1)
    prepare(0)
    for t in range(TURN - 1):
        blocks[BLOCKS + t] = blocks[t]
    score(0, PER - STEP)
    distant(2)
    complete(1)
    prepare(1)
    score(PER - STEP, 2 * PER - STEP)
    complete(2)
    prepare(2)
    score(2 * PER - STEP, BLOCKS)

    curve_rows = jnp.concatenate([curves[...]] * TURN, axis=0)
    square_rows = jnp.concatenate([squares[...] * twice(noise_row)] * TURN, axis=0)
    normal = dot_nt(powers[...], curve_rows, HIGHEST)
    offset = 0.5 * dot_nt(jnp.ones((8, 128), F32), square_rows, HIGHEST)
    bias = 0.5 * normal + offset[:1, :]

    def over_turns(v, op):
        v = op(v, pltpu.roll(v, 64, 1))
        return op(v, pltpu.roll(v, 128, 1))

    top = None
    for s in range(SHIFT):
        value = cross[pl.ds(s * HALF, HALF), :] - bias
        cross[pl.ds(s * HALF, HALF), :] = value
        value = jnp.max(value, axis=0, keepdims=True)
        top = value if top is None else jnp.maximum(top, value)
    top = over_turns(jnp.broadcast_to(top, (8, WIDE)), jnp.maximum)
    norm = None
    for s in range(SHIFT):
        value = jnp.exp(cross[pl.ds(s * HALF, HALF), :] - top[:1, :])
        cross[pl.ds(s * HALF, HALF), :] = value
        value = jnp.sum(value, axis=0, keepdims=True)
        norm = value if norm is None else norm + value
    norm = over_turns(jnp.broadcast_to(norm, (8, WIDE)), jnp.add)
    row = lax.broadcasted_iota(jnp.int32, (8, WIDE), 0)
    own_stats[...] = jnp.where(row < 4, top, norm)

    stat_copies = [remote(own_stats, stats.at[o - 1], st_send.at[o - 1], st_recv.at[o - 1], peer(o)) for o in range(1, SLOTS)]
    for copy in stat_copies:
        copy.start()
    for copy in stat_copies:
        copy.wait_recv()
    top, norm = top[:1, :], norm[:1, :]
    best = top
    for o in range(SLOTS - 1):
        best = jnp.maximum(best, stats[o, 0:1, :])
    mine = jnp.exp(top - best)
    norm = norm * mine
    for o in range(SLOTS - 1):
        norm = norm + stats[o, 4:5, :] * jnp.exp(stats[o, 0:1, :] - best)
    scale = mine / norm

    mass = None
    for s in range(SHIFT):
        value = (cross[pl.ds(s * HALF, HALF), :] * scale).astype(BF16)
        weights[pl.ds(s * HALF, HALF), :] = value
        value = value.astype(F32)
        mass = value if mass is None else mass + value
    denom = dot_nn(mass, curve_rows, HIGHEST)
    for k in range(4):
        bottoms[k] = denom[k * PIECE:(k + 1) * PIECE]

    def accumulate(j):
        for m in range(SHIFT):
            value = dot_nn(weights[...], blocks[pl.ds(4 * m + j, TURN)].reshape(TURN * PART, WIDE))
            for s in range(SHIFT):
                piece = value[s * HALF:(s + 1) * HALF]
                if m == 0:
                    numer[j, s] = piece
                else:
                    numer[j, (m + s) % SHIFT] += piece

    def lanes(m):
        return pl.ds(m * WIDE, WIDE)

    ends = pl.ds(QUARTER, 128), pl.ds(QUARTER + 128, 128)

    def finish_ends(ref, index, value):
        high, low = split(value)
        ref[index, :, ends[0]] = high
        ref[index, :, ends[1]] = low

    def read_ends(ref, index):
        return ref[index, :, ends[0]].astype(F32) + ref[index, :, ends[1]].astype(F32)

    def pack(j, ks):
        for k in ks:
            for m in range(SHIFT):
                parts[j, k, :, lanes(m)] = numer[j, m, pl.ds(k * PIECE, PIECE), :].astype(BF16)
            high, low = split(bottoms[k])
            parts[j, k, :, ends[0]] = high
            parts[j, k, :, ends[1]] = low

    def pass_on(j, ks, near):
        for k in ks:
            for m in range(SHIFT):
                fwd[k, :, lanes(m)] = (
                    numer[j, m, pl.ds(k * PIECE, PIECE), :] + near[k - ks[0], :, lanes(m)].astype(F32)).astype(BF16)
            finish_ends(fwd, k, bottoms[k] + read_ends(near, k - ks[0]))

    reduced = []

    def reduce_copy(src, dst, target):
        i = len(reduced)
        reduced.append(remote(src, dst, rs_send.at[i], rs_recv.at[i], target))
        reduced[i].start()
        return reduced[i]

    low, high = pl.ds(0, 2), pl.ds(2, 2)
    accumulate(opp1)
    pack(opp1, range(4))
    a = reduce_copy(parts.at[opp1, low], far_low, to_r1)
    b = reduce_copy(parts.at[opp1, high], far_high, to_l1)
    accumulate(right1)
    pack(right1, (2, 3))
    c = reduce_copy(parts.at[right1, high], plain.at[high], to_r1)
    accumulate(left1)
    pack(left1, (0, 1))
    d = reduce_copy(parts.at[left1, low], plain.at[low], to_l1)
    a.wait_recv()
    pass_on(right1, (0, 1), far_low)
    e = reduce_copy(fwd.at[low], summed.at[low], to_r1)
    b.wait_recv()
    pass_on(left1, (2, 3), far_high)
    f = reduce_copy(fwd.at[high], summed.at[high], to_l1)
    accumulate(q1)
    for copy in (c, d, e, f):
        copy.wait_recv()

    def settle(k):
        rows = pl.ds(pl.multiple_of(k * PIECE, PIECE), PIECE)
        for m in range(SHIFT):
            value = (numer[q1, m, rows, :] + plain[k, :, lanes(m)].astype(F32)) + summed[k, :, lanes(m)].astype(F32)
            total[k, :, lanes(m)] = value
            ready[k, :, lanes(m)] = value.astype(BF16)
        value = bottoms[k] + read_ends(plain, k) + read_ends(summed, k)
        total_bottom[k] = value
        finish_ends(ready, k, value)

    left, right = pl.ds(0, CUT), pl.ds(CUT, CUT)
    rest = QUARTER - CUT
    settle(opp2)
    a2 = reduce_copy(ready.at[opp2, :, left], two_a, to_r2)
    b2 = reduce_copy(ready.at[opp2, :, right], two_b, to_l2)
    settle(right2)
    c2 = reduce_copy(ready.at[right2, :, right], two_c, to_r2)
    settle(left2)
    d2 = reduce_copy(ready.at[left2, :, left], two_d, to_l2)
    settle(q2)

    def bottom_of(ref):
        return ref[:, pl.ds(rest, 128)].astype(F32) + ref[:, pl.ds(rest + 128, 128)].astype(F32)

    a2.wait_recv()
    two_fa[...] = (total[right2, :, left] + two_a[...].astype(F32)).astype(BF16)
    e2 = reduce_copy(two_fa, two_e, to_r2)
    b2.wait_recv()
    two_fb[:, pl.ds(0, rest)] = (total[left2, :, pl.ds(CUT, rest)] + two_b[:, pl.ds(0, rest)].astype(F32)).astype(BF16)
    hi, lo = split(total_bottom[left2] + bottom_of(two_b))
    two_fb[:, pl.ds(rest, 128)] = hi
    two_fb[:, pl.ds(rest + 128, 128)] = lo
    f2 = reduce_copy(two_fb, two_f, to_l2)
    for copy in (c2, d2, f2, e2):
        copy.wait_recv()
    inverse_rows = (total_bottom[q2] + bottom_of(two_c)) + bottom_of(two_f) + twice(reg[...])
    first_part = total[q2, :, left] + two_d[...].astype(F32) + two_e[...].astype(F32)
    second_part = (total[q2, :, pl.ds(CUT, rest)] + two_c[:, pl.ds(0, rest)].astype(F32)
                   + two_f[:, pl.ds(0, rest)].astype(F32))
    value = jnp.concatenate([first_part, second_part], axis=1)

    def level_of(half):
        return y_hi if half == 0 else 1 - y_hi

    def block(half, v1, v2, start=0, count=QUARTER):
        return pieces.at[level_of(half) * 4 + v2, v1, :, pl.ds(start, count)]

    pieces[y_hi * 4 + q2, q1] = (value / jnp.concatenate([inverse_rows] * (QUARTER // 128), axis=1)).astype(BF16)

    def deliver(half, v1, v2):
        index = level_of(half) * 4 + v2
        rows = pl.ds(pl.multiple_of(index * PIECE, PIECE), PIECE)
        for m in range(SHIFT):
            place = pl.ds(pl.multiple_of(v1 * WIDE + m * 4 * WIDE, WIDE), WIDE)
            out[rows, place] = pieces[index, v1, :, lanes(m)].astype(F32)

    copies = {}

    def gather(name, half, v1, v2, target, start=0, count=QUARTER):
        ref = block(half, v1, v2, start, count)
        i = len(copies)
        copies[name] = remote(ref, ref, ag_send.at[i], ag_recv.at[i], target)
        copies[name].start()

    def arrived(*names):
        for name in names:
            copies[name].wait_recv()

    mid = QUARTER // 2

    def spread(half, i, v2):
        gather((half, "right", i), half, q1, v2, to_r1)
        gather((half, "left", i), half, q1, v2, to_l1)

    def begin(half):
        gather((half, "r2"), half, q1, q2, to_r2)
        gather((half, "l2"), half, q1, q2, to_l2)
        spread(half, 0, q2)
        deliver(half, q1, q2)

    def middle(half):
        arrived((half, "r2"))
        gather((half, "fr2"), half, q1, left2, to_r2, 0, mid)
        spread(half, 1, left2)
        arrived((half, "l2"))
        gather((half, "fl2"), half, q1, right2, to_l2, mid, mid)
        spread(half, 2, right2)
        deliver(half, q1, left2)
        deliver(half, q1, right2)

    def last(half):
        arrived((half, "fr2"), (half, "fl2"))
        spread(half, 3, opp2)
        deliver(half, q1, opp2)

    def relay(half, i, v2):
        arrived((half, "right", i), (half, "left", i))
        if i in (0, 3):
            gather((half, "fright", i), half, left1, v2, to_r1)
        else:
            gather((half, "fleft", i), half, right1, v2, to_l1)
        deliver(half, left1, v2)
        deliver(half, right1, v2)

    gather("y", 0, q1, q2, to_y)
    begin(0)
    middle(0)
    arrived("y")
    begin(1)
    last(0)
    relay(0, 0, q2)
    middle(1)
    relay(0, 1, left2)
    relay(0, 2, right2)
    last(1)
    relay(0, 3, opp2)
    relay(1, 0, q2)
    relay(1, 1, left2)
    relay(1, 2, right2)
    relay(1, 3, opp2)
    for half in (0, 1):
        for i, v2, way in ((0, q2, "fright"), (1, left2, "fleft"), (2, right2, "fleft"), (3, opp2, "fright")):
            arrived((half, way, i))
            deliver(half, opp1, v2)
    for copy in list(moves.values()) + ctf_copies + stat_copies + reduced + list(copies.values()):
        copy.wait_send()


def body(images, ctf, refs, noise_inv, reg):
    hbm = pl.BlockSpec(memory_space=pltpu.MemorySpace.HBM)
    dma = pltpu.SemaphoreType.DMA
    vmem = pltpu.VMEM
    near = vmem((2, PIECE, FULL), BF16)
    four = vmem((4, PIECE, FULL), BF16)
    two = vmem((PIECE, CUT), BF16)
    return pl.pallas_call(
        kernel,
        out_shape=jax.ShapeDtypeStruct((2 * HALF, PIX), F32),
        in_specs=[hbm] * 5,
        out_specs=pl.BlockSpec(memory_space=pltpu.VMEM),
        scratch_shapes=[
            vmem((SLOTS, ROWS, PIX), BF16),
            vmem((SLOTS, ROWS, CYCLES), BF16),
            vmem((BLOCKS + TURN - 1, PART, WIDE), BF16),
            vmem((4, 2 * SHIFT - 1, HALF, WIDE), BF16),
            vmem((1, CYCLES), F32),
            vmem((1, CYCLES), F32),
            vmem((PART, 128), F32),
            vmem((PART, 128), F32),
            vmem((PART, 128), F32),
            vmem((HALF, 128), F32),
            vmem((SHIFT * HALF, TURN * PART), F32),
            vmem((SHIFT * HALF, TURN * PART), BF16),
            vmem((SLOTS - 1, 8, WIDE), F32),
            vmem((8, WIDE), F32),
            vmem((4, SHIFT, HALF, WIDE), F32),
            vmem((4, PIECE, 128), F32),
            vmem((4, 4, PIECE, FULL), BF16),
            near, near, four, four, four,
            vmem((4, PIECE, QUARTER), F32),
            vmem((4, PIECE, 128), F32),
            four,
            two, two, two, two, two, two, two, two,
            vmem((8, 4, PIECE, QUARTER), BF16),
            dma((9 * CHUNKS,)), dma((9 * CHUNKS,)), dma((7,)), dma((7,)), dma((7,)), dma((7,)), dma((4,)),
            dma((4 * (2 * SHIFT - 1),)), dma((12,)), dma((12,)), dma((33,)), dma((33,)),
        ],
        compiler_params=pltpu.CompilerParams(
            collective_id=0, has_side_effects=True, vmem_limit_bytes=40 * 1024 * 1024),
        name="step",
    )(images, ctf, refs, noise_inv.reshape(1, CYCLES), reg.reshape(1, CYCLES))


def solution(mesh):
    in_specs = (P(("cls", "grp"), None), P(("cls", "grp"), None), P("cls", None), P(), P())
    return jax.shard_map(body, mesh=mesh, in_specs=in_specs, out_specs=P("cls", None), check_vma=False)
```

profile of v0, /device:TPU:0, one launch (start us, length us, event | category | flops | bytes accessed | tf_op | source)
XLA Modules:
  0.0 74.6 jit_solution(417137944921066961)
XLA Ops:
  0.0 0.0 copy-start
  0.0 1.7 %copy-done = bf16[128,9216]{1,0:T(8,128)(2,1)S(1)} copy-done((bf16[128,9216]{1,0:T(8,128)(2,1)S(1)}, bf16[128,9216]{1,0:T(8,128)(2,1)}, u32[]{:S(2)}) %copy-start) | copy-done | bytes 2359320
  1.7 0.0 copy-start.1
  1.7 0.9 %copy-done.1 = bf16[8,9216]{1,0:T(8,128)(2,1)S(1)} copy-done((bf16[8,9216]{1,0:T(8,128)(2,1)S(1)}, bf16[8,9216]{1,0:T(8,128)(2,1)}, u32[]{:S(2)}) %copy-start.1) | copy-done | bytes 147480
  2.6 0.0 copy-start.2
  2.6 0.7 copy-done.2
  3.3 0.0 copy-start.3
  3.3 0.7 copy-done.3
  3.9 0.0 copy-start.4
  3.9 0.7 copy-done.4
  4.6 67.8 %step.1 = f32[128,9216]{1,0:T(8,128)S(1)} custom-call(bf16[8,9216]{1,0:T(8,128)(2,1)S(1)} %copy-done.1, bf16[8,64]{1,0:T(8,128)(2,1)S(1)} %copy-done.2, bf16[128,9216]{1,0:T(8,128)(2,1)S(1)} %copy-done, f32[1,64]{1,0:T(1,128)S(1)} %bitcast.2, f32[1,64]{1,0:T(1,128)S(1)} %bitcast.3), custom_call_target="tpu_custom_call" | custom-call | tf_op jit(solution)/shard_map/step/pallas_call | solution.py:495
  72.4 2.2 %copy.7 = f32[128,9216]{1,0:T(8,128)} copy(f32[128,9216]{1,0:T(8,128)S(1)} %step.1) | data formatting | bytes 9437184
Async XLA Ops:
  0.0 1.7 %copy-start = (bf16[128,9216]{1,0:T(8,128)(2,1)S(1)}, bf16[128,9216]{1,0:T(8,128)(2,1)}, u32[]{:S(2)}) copy-start(bf16[128,9216]{1,0:T(8,128)(2,1)} %refs.1) | copy-start | bytes 7077892
  1.7 0.9 %copy-start.1 = (bf16[8,9216]{1,0:T(8,128)(2,1)S(1)}, bf16[8,9216]{1,0:T(8,128)(2,1)}, u32[]{:S(2)}) copy-start(bf16[8,9216]{1,0:T(8,128)(2,1)} %images.1) | copy-start | bytes 442372
  2.6 0.7 copy-start.2
  3.3 0.7 copy-start.3
  3.9 0.7 copy-start.4
where the time goes:
time: 74.8 us; the launch traced here: 74.6 us
  Pallas kernels  67.8 us (91%)
  local copies, waits for them, and re-layouts  6.75 us (9%)
    pallas_call x1, Pallas kernels, body(): pl.pallas_call(kernel, out_shape=jax.ShapeDtypeStruct((2 * HALF, PIX), F3...  67.8 us
    unnamed x11, local copies, waits for them, and re-layouts  6.75 us

commit v1 on v0

--- a/solution.py
+++ b/solution.py
@@ -23,11 +23,10 @@
 PIECE = 16
 QUARTER = PIX // 4
 FULL = QUARTER + 256
-CUT = FULL // 2
 CHUNKS = 3
 CHUNK = PIX // CHUNKS
 PER = BLOCKS // CHUNKS
-STEP = 3
+STEP = 4
 
 
 def ring(v, step):
@@ -63,7 +62,7 @@
 
 def kernel(images, ctf, refs, noise_hbm, reg_hbm, out, gathered, ctfs, blocks, classes, noise, reg, factors, curves,
            squares, powers, cross, weights, stats, own_stats, numer, bottoms, parts, far_low, far_high, plain, summed,
-           fwd, total, total_bottom, ready, two_a, two_b, two_c, two_d, two_e, two_f, two_fa, two_fb, pieces,
+           fwd, total, total_bottom, ready, two_left, two_right, two_far, pieces,
            img_send, img_recv, ctf_send, ctf_recv, st_send, st_recv, loc_sem, ref_sem, rs_send, rs_recv, ag_send, ag_recv):
     cls = lax.axis_index("cls")
     grp = lax.axis_index("grp")
@@ -84,6 +83,7 @@
     right2, left2, opp2 = ring(q2, 1), ring(q2, 3), ring(q2, 2)
     to_r1, to_l1 = at(right1, q2), at(left1, q2)
     to_r2, to_l2 = at(q1, right2), at(q1, left2)
+    to_o1, to_o2 = at(opp1, q2), at(q1, opp2)
     to_y = device(x, far, z, core)
 
     def peer(o):
@@ -93,7 +93,7 @@
     barrier = pltpu.get_barrier_semaphore()
     for o in range(1, SLOTS):
         pl.semaphore_signal(barrier, inc=1, device_id=peer(o), device_id_type=MESH)
-    for target in (to_r1, to_l1, to_r2, to_l2):
+    for target in (to_r1, to_l1, to_o1, to_r2, to_l2, to_o2):
         pl.semaphore_signal(barrier, inc=1, device_id=target, device_id_type=MESH)
 
     local = [
@@ -113,67 +113,43 @@
                 refs.at[pl.ds(first, HALF), pl.ds(b * WIDE, WIDE)], classes.at[j, m], ref_sem.at[len(ref_copies)]))
             ref_copies[-1].start()
 
-    pl.semaphore_wait(barrier, SLOTS + 3)
+    pl.semaphore_wait(barrier, SLOTS + 5)
 
     sibling = device(x, y, z, 1 - core)
     above = device(x, up, z, core)
     below = device(x, down, z, core)
+    farthest = device(x, far, z, core)
     slot_down, slot_up, slot_far = down * 2 + core, up * 2 + core, far * 2 + core
     moves = {}
 
     def move(c, i):
-        if i < 3:
-            slot, lo, size, target = me, 0, CHUNK, (above, below, sibling)[i]
-        elif i == 3:
-            slot, lo, size, target = slot_down, 0, CHUNK // 2, above
-        elif i == 4:
-            slot, lo, size, target = slot_down, 0, CHUNK, sibling
-        elif i == 5:
-            slot, lo, size, target = slot_up, CHUNK // 2, CHUNK // 2, below
-        elif i == 6:
-            slot, lo, size, target = slot_up, 0, CHUNK, sibling
-        else:
-            slot, lo, size, target = slot_far, (i - 7) * (CHUNK // 2), CHUNK // 2, sibling
-        lanes = pl.ds(c * CHUNK + lo, size)
-        src = images.at[:, lanes] if i < 3 else gathered.at[slot, :, lanes]
-        moves[c, i] = remote(src, gathered.at[slot, :, lanes], img_send.at[9 * c + i], img_recv.at[9 * c + i], target)
+        slot = (me, me, me, me, slot_far, slot_down, slot_up)[i]
+        target = (farthest, above, below, sibling, sibling, sibling, sibling)[i]
+        lanes = pl.ds(c * CHUNK, CHUNK)
+        src = images.at[:, lanes] if i < 4 else gathered.at[slot, :, lanes]
+        moves[c, i] = remote(src, gathered.at[slot, :, lanes], img_send.at[7 * c + i], img_recv.at[7 * c + i], target)
         moves[c, i].start()
 
-    def neighbours(c):
-        moves[c, 0].wait_recv()
-        move(c, 3)
-        move(c, 4)
-        moves[c, 1].wait_recv()
-        move(c, 5)
-        move(c, 6)
-
-    def distant(c):
-        moves[c, 3].wait_recv()
-        move(c, 7)
-        moves[c, 5].wait_recv()
-        move(c, 8)
+    def share(c):
+        for arriving, passing in ((1, 5), (2, 6), (0, 4)):
+            moves[c, arriving].wait_recv()
+            move(c, passing)
 
     def complete(c):
-        for i in (2, 4, 6, 7, 8):
+        for i in range(3, 7):
             moves[c, i].wait_recv()
 
-    move(0, 0)
-    move(0, 1)
-    move(1, 0)
-    move(1, 1)
+    for i in range(3):
+        move(0, i)
     ctf_copies = [remote(ctf, ctfs.at[me], ctf_send.at[o - 1], ctf_recv.at[o - 1], peer(o)) for o in range(1, SLOTS)]
     for copy in ctf_copies:
         copy.start()
-    move(0, 2)
+    for c, i in ((0, 3), (1, 0), (1, 1), (1, 2), (1, 3), (2, 0), (2, 1), (2, 2), (2, 3)):
+        move(c, i)
     cross[...] = jnp.zeros_like(cross)
     squares[...] = jnp.zeros_like(squares)
     for copy in local:
         copy.wait()
-    neighbours(0)
-    move(2, 0)
-    move(2, 1)
-    move(1, 2)
-    move(2, 2)
     for copy in ref_copies:
         copy.wait()
     powers[...] = jnp.zeros_like(powers)
@@ -221,17 +197,15 @@
                 right.append(blocks[pl.ds(b, TURN)].reshape(TURN * PART, WIDE))
             cross[...] += dot_nt(jnp.concatenate(left, axis=1), jnp.concatenate(right, axis=1))
 
-    neighbours(1)
-    distant(0)
+    share(0)
     complete(0)
-    neighbours(2)
-    distant(1)
     prepare(0)
     for t in range(TURN - 1):
         blocks[BLOCKS + t] = blocks[t]
+    share(1)
     score(0, PER - STEP)
-    distant(2)
     complete(1)
+    share(2)
     prepare(1)
     score(PER - STEP, 2 * PER - STEP)
     complete(2)
@@ -367,44 +341,25 @@
         total_bottom[k] = value
         finish_ends(ready, k, value)
 
-    left, right = pl.ds(0, CUT), pl.ds(CUT, CUT)
-    rest = QUARTER - CUT
     settle(opp2)
-    a2 = reduce_copy(ready.at[opp2, :, left], two_a, to_r2)
-    b2 = reduce_copy(ready.at[opp2, :, right], two_b, to_l2)
+    far2 = reduce_copy(ready.at[opp2], two_far, to_o2)
     settle(right2)
-    c2 = reduce_copy(ready.at[right2, :, right], two_c, to_r2)
+    up2 = reduce_copy(ready.at[right2], two_left, to_r2)
     settle(left2)
-    d2 = reduce_copy(ready.at[left2, :, left], two_d, to_l2)
+    down2 = reduce_copy(ready.at[left2], two_right, to_l2)
     settle(q2)
-
-    def bottom_of(ref):
-        return ref[:, pl.ds(rest, 128)].astype(F32) + ref[:, pl.ds(rest + 128, 128)].astype(F32)
-
-    a2.wait_recv()
-    two_fa[...] = (total[right2, :, left] + two_a[...].astype(F32)).astype(BF16)
-    e2 = reduce_copy(two_fa, two_e, to_r2)
-    b2.wait_recv()
-    two_fb[:, pl.ds(0, rest)] = (total[left2, :, pl.ds(CUT, rest)] + two_b[:, pl.ds(0, rest)].astype(F32)).astype(BF16)
-    hi, lo = split(total_bottom[left2] + bottom_of(two_b))
-    two_fb[:, pl.ds(rest, 128)] = hi
-    two_fb[:, pl.ds(rest + 128, 128)] = lo
-    f2 = reduce_copy(two_fb, two_f, to_l2)
-    for copy in (c2, d2, f2, e2):
+    for copy in (up2, down2, far2):
         copy.wait_recv()
-    inverse_rows = (total_bottom[q2] + bottom_of(two_c)) + bottom_of(two_f) + twice(reg[...])
-    first_part = total[q2, :, left] + two_d[...].astype(F32) + two_e[...].astype(F32)
-    second_part = (total[q2, :, pl.ds(CUT, rest)] + two_c[:, pl.ds(0, rest)].astype(F32)
-                   + two_f[:, pl.ds(0, rest)].astype(F32))
-    value = jnp.concatenate([first_part, second_part], axis=1)
+    bottom = total_bottom[q2] + twice(reg[...])
+    value = total[q2]
+    for ref in (two_left, two_right, two_far):
+        bottom = bottom + (ref[:, ends[0]].astype(F32) + ref[:, ends[1]].astype(F32))
+        value = value + ref[:, pl.ds(0, QUARTER)].astype(F32)
 
     def level_of(half):
         return y_hi if half == 0 else 1 - y_hi
 
-    def block(half, v1, v2, start=0, count=QUARTER):
-        return pieces.at[level_of(half) * 4 + v2, v1, :, pl.ds(start, count)]
-
-    pieces[y_hi * 4 + q2, q1] = (value / jnp.concatenate([inverse_rows] * (QUARTER // 128), axis=1)).astype(BF16)
+    pieces[y_hi * 4 + q2, q1] = (value / jnp.concatenate([bottom] * (QUARTER // 128), axis=1)).astype(BF16)
 
     def deliver(half, v1, v2):
         index = level_of(half) * 4 + v2
@@ -415,8 +370,8 @@
 
     copies = {}
 
-    def gather(name, half, v1, v2, target, start=0, count=QUARTER):
-        ref = block(half, v1, v2, start, count)
+    def gather(name, half, v1, v2, target):
+        ref = pieces.at[level_of(half) * 4 + v2, v1]
         i = len(copies)
         copies[name] = remote(ref, ref, ag_send.at[i], ag_recv.at[i], target)
         copies[name].start()
@@ -425,62 +380,73 @@
         for name in names:
             copies[name].wait_recv()
 
-    mid = QUARTER // 2
-
-    def spread(half, i, v2):
+    def across(half):
+        gather((half, "o2"), half, q1, q2, to_o2)
+        gather((half, "r2"), half, q1, q2, to_r2)
+        gather((half, "l2"), half, q1, q2, to_l2)
+
+    def spread(half, i, v2, direct=False):
+        if direct:
+            gather((half, "opp", i), half, q1, v2, to_o1)
         gather((half, "right", i), half, q1, v2, to_r1)
         gather((half, "left", i), half, q1, v2, to_l1)
 
-    def begin(half):
-        gather((half, "r2"), half, q1, q2, to_r2)
-        gather((half, "l2"), half, q1, q2, to_l2)
-        spread(half, 0, q2)
-        deliver(half, q1, q2)
-
-    def middle(half):
-        arrived((half, "r2"))
-        gather((half, "fr2"), half, q1, left2, to_r2, 0, mid)
-        spread(half, 1, left2)
-        arrived((half, "l2"))
-        gather((half, "fl2"), half, q1, right2, to_l2, mid, mid)
-        spread(half, 2, right2)
-        deliver(half, q1, left2)
-        deliver(half, q1, right2)
-
-    def last(half):
-        arrived((half, "fr2"), (half, "fl2"))
-        spread(half, 3, opp2)
-        deliver(half, q1, opp2)
-
     def relay(half, i, v2):
-        arrived((half, "right", i), (half, "left", i))
         if i in (0, 3):
-            gather((half, "fright", i), half, left1, v2, to_r1)
+            arrived((half, "right", i))
+            gather((half, "opp", i), half, left1, v2, to_r1)
+            arrived((half, "left", i))
         else:
-            gather((half, "fleft", i), half, right1, v2, to_l1)
-        deliver(half, left1, v2)
-        deliver(half, right1, v2)
+            arrived((half, "left", i))
+            gather((half, "opp", i), half, right1, v2, to_l1)
+            arrived((half, "right", i))
 
     gather("y", 0, q1, q2, to_y)
-    begin(0)
-    middle(0)
+    across(0)
+    spread(0, 0, q2)
+    deliver(0, q1, q2)
+    arrived((0, "r2"))
+    spread(0, 1, left2)
+    arrived((0, "l2"))
+    spread(0, 2, right2)
     arrived("y")
-    begin(1)
-    last(0)
+    across(1)
+    spread(1, 0, q2)
     relay(0, 0, q2)
-    middle(1)
+    arrived((0, "o2"))
+    spread(0, 3, opp2)
+    for v1, v2 in ((q1, left2), (q1, right2), (q1, opp2), (left1, q2), (right1, q2)):
+        deliver(0, v1, v2)
+    deliver(1, q1, q2)
     relay(0, 1, left2)
     relay(0, 2, right2)
-    last(1)
+    arrived((1, "r2"))
+    spread(1, 1, left2, True)
+    arrived((1, "l2"))
+    spread(1, 2, right2, True)
+    relay(1, 0, q2)
+    arrived((1, "o2"))
+    spread(1, 3, opp2, True)
     relay(0, 3, opp2)
-    relay(1, 0, q2)
-    relay(1, 1, left2)
-    relay(1, 2, right2)
-    relay(1, 3, opp2)
-    for half in (0, 1):
-        for i, v2, way in ((0, q2, "fright"), (1, left2, "fleft"), (2, right2, "fleft"), (3, opp2, "fright")):
-            arrived((half, way, i))
-            deliver(half, opp1, v2)
+    for v1 in (left1, right1):
+        for v2 in (left2, right2, opp2):
+            deliver(0, v1, v2)
+    for v2 in (left2, right2, opp2):
+        deliver(1, q1, v2)
+    for v1 in (left1, right1):
+        deliver(1, v1, q2)
+    for i, v2 in ((0, q2), (1, left2), (2, right2), (3, opp2)):
+        arrived((0, "opp", i))
+        deliver(0, opp1, v2)
+    arrived((1, "opp", 0))
+    deliver(1, opp1, q2)
+    for i, v2 in ((1, left2), (2, right2), (3, opp2)):
+        arrived((1, "right", i), (1, "left", i))
+        deliver(1, left1, v2)
+        deliver(1, right1, v2)
+    for i, v2 in ((1, left2), (2, right2), (3, opp2)):
+        arrived((1, "opp", i))
+        deliver(1, opp1, v2)
     for copy in list(moves.values()) + ctf_copies + stat_copies + reduced + list(copies.values()):
         copy.wait_send()
 
@@ -491,7 +457,7 @@
     vmem = pltpu.VMEM
     near = vmem((2, PIECE, FULL), BF16)
     four = vmem((4, PIECE, FULL), BF16)
-    two = vmem((PIECE, CUT), BF16)
+    two = vmem((PIECE, FULL), BF16)
     return pl.pallas_call(
         kernel,
         out_shape=jax.ShapeDtypeStruct((2 * HALF, PIX), F32),
@@ -519,15 +485,15 @@
             vmem((4, PIECE, QUARTER), F32),
             vmem((4, PIECE, 128), F32),
             four,
-            two, two, two, two, two, two, two, two,
+            two, two, two,
             vmem((8, 4, PIECE, QUARTER), BF16),
-            dma((9 * CHUNKS,)), dma((9 * CHUNKS,)), dma((7,)), dma((7,)), dma((7,)), dma((7,)), dma((4,)),
-            dma((4 * (2 * SHIFT - 1),)), dma((12,)), dma((12,)), dma((33,)), dma((33,)),
+            dma((7 * CHUNKS,)), dma((7 * CHUNKS,)), dma((7,)), dma((7,)), dma((7,)), dma((7,)), dma((4,)),
+            dma((4 * (2 * SHIFT - 1),)), dma((9,)), dma((9,)), dma((31,)), dma((31,)),
         ],
         compiler_params=pltpu.CompilerParams(
             collective_id=0, has_side_effects=True, vmem_limit_bytes=40 * 1024 * 1024),
         name="step",
-    )(images, ctf, refs, noise_inv.reshape(1, CYCLES), reg.reshape(1, CYCLES))
+    )(*[pltpu.with_memory_space_constraint(v, pltpu.MemorySpace.HBM) for v in (images, ctf, refs, noise_inv.reshape(1, CYCLES), reg.reshape(1, CYCLES))])
 
 
 def solution(mesh):

time: 74.8 us -> 64.7 us (0.86)
  Pallas kernels: 67.8 us -> 62.4 us
  local copies, waits for them, and re-layouts: 6.75 us -> 2.19 us
    pallas_call x1, Pallas kernels: 67.8 us -> 62.4 us  [body(): pl.pallas_call(kernel, out_shape=jax.ShapeDtypeStruct((2 * HALF, PIX), F3...]
    unnamed x11 -> x1, local copies, waits for them, and re-layouts: 6.75 us -> 2.19 us
where the time goes in v1:
time: 64.7 us; the launch traced here: 64.6 us
  Pallas kernels  62.4 us (96%)
  local copies, waits for them, and re-layouts  2.19 us (3%)
    pallas_call x1, Pallas kernels, body(): pl.pallas_call(kernel, out_shape=jax.ShapeDtypeStruct((2 * HALF, PIX), F3...  62.4 us
    unnamed x1, local copies, waits for them, and re-layouts  2.19 us

profile of v1, /device:TPU:0, one launch (start us, length us, event | category | flops | bytes accessed | tf_op | source)
XLA Modules:
  0.0 64.6 jit_solution(13727751656680103573)
XLA Ops:
  0.0 62.4 %step.1 = f32[128,9216]{1,0:T(8,128)S(1)} custom-call(bf16[8,9216]{1,0:T(8,128)(2,1)} %images.1, bf16[8,64]{1,0:T(8,128)(2,1)} %ctf.1, bf16[128,9216]{1,0:T(8,128)(2,1)} %refs.1, f32[1,64]{1,0:T(1,128)} %bitcast.2, f32[1,64]{1,0:T(1,128)} %bitcast.3), custom_call_target="tpu_custom_call" | custom-call | tf_op jit(solution)/shard_map/step/pallas_call | solution.py:461
  62.4 2.2 %copy.7 = f32[128,9216]{1,0:T(8,128)} copy(f32[128,9216]{1,0:T(8,128)S(1)} %step.1) | data formatting | bytes 9437184
